TPU v7x, 32 devices: a whole 2x2x4 slice. The times are simulated.
32 devices in a mesh: ab: 4 (over y, x), cd: 4 (over z), ij: 2 (over core).
Axes of the slice: x: 2, y: 2, z: 4, core: 2. Of those that a mesh axis runs over, the one named last changes fastest.
Arguments:
- amplitudes: float32 [512, 4096], P('ij', ('cd', 'ab')), may hold values from -6 to 6
- integrals: float32 [256, 256, 256], P(('ab', 'cd')), may hold values from -0.375 to 0.375
- tile_row: int32 [256], P(('ab', 'cd')), may hold values from 0 to 3, as said below
- tile_col: int32 [256], P(('ab', 'cd')), may hold values from 0 to 3
- tile_count: int32 [16], P(('ab', 'cd')), may hold values from 1 to 16, as said below
Outputs:
- residual: float32 [512, 4, 16, 64], P('ij', 'ab', 'cd')
Inputs may be any that keep to these rules, and one draw needn't show every extreme that they name: Within one slab the 16 slots name distinct (tile_row, tile_col) pairs. `tile_count`: in every draw some slab has all 16 slots live.
All inputs are finite; a program needn't handle non-finite values.
Results may differ from a plain program's by a relative error of at most 0.0003.
Values sent between devices are 32-bit elements; how exact they have to be, the bound alone decides.
A program may use at most 128 MiB of HBM per device.

v0:
```python
import math
import jax
import jax.numpy as jnp
from jax import lax
from jax.sharding import PartitionSpec as P


def from_partner(block, axis, bit):
    count = lax.axis_size(axis)
    route = []
    for low in range(count):
        high = low | 1 << bit
        if high != low and high < count:
            route += [(low, high), (high, low)]
    return lax.ppermute(block, axis, route)


def place_rows(chosen, tile_rows, row_picks, block_size):
    terms = jnp.einsum("okf,kef->oke", chosen, tile_rows, precision=lax.Precision.HIGHEST)
    occ_dev, slots, width = terms.shape
    terms = terms.reshape(occ_dev, slots, width // block_size, block_size)
    placed = jnp.einsum("rk,okab->aorb", row_picks, terms, precision=lax.Precision.HIGHEST)
    return placed.reshape(width // block_size, occ_dev, row_picks.shape[0] * block_size)


def per_device(amplitudes, integrals, tile_row, tile_col, tile_count):
    occ_dev = amplitudes.shape[0]
    slots = integrals.shape[0]
    tile_size = integrals.shape[1]
    block_size = math.isqrt(tile_size)
    blocks = lax.axis_size("ab")
    cd_size = lax.axis_size("cd")
    group_size = block_size // cd_size
    live_count = tile_count[0]
    live = jnp.arange(slots, dtype=jnp.int32) < live_count
    row_picks = (
        (tile_row[None, :] == jnp.arange(blocks, dtype=jnp.int32)[:, None]) & live[None, :]
    ).astype(jnp.float32)
    gathered = lax.all_gather(amplitudes, "ab", axis=1, tiled=True)
    columns = gathered.reshape(occ_dev, -1, tile_size)
    chosen = jnp.take(columns, tile_col, axis=1)
    partial_value = place_rows(chosen, integrals, row_picks, block_size)
    summed = lax.psum_scatter(partial_value, "cd", scatter_dimension=0, tiled=True)
    direct = jnp.transpose(summed, (1, 0, 2))
    outgoing = summed.reshape(group_size, occ_dev, blocks, cd_size, group_size)
    outgoing = jnp.transpose(outgoing, (2, 3, 1, 0, 4))
    arrived = lax.all_to_all(
        outgoing.reshape(blocks * cd_size, occ_dev * group_size * group_size),
        ("ab", "cd"),
        split_axis=0,
        concat_axis=0,
        tiled=True,
    )
    arrived = arrived.reshape(blocks, cd_size, occ_dev, group_size, group_size)
    mirrored = jnp.transpose(arrived, (2, 4, 0, 1, 3)).reshape(
        occ_dev, group_size, blocks * block_size
    )
    partner = from_partner(mirrored, "ij", 0)
    return (direct + partner).reshape(occ_dev, 1, group_size, blocks * block_size)


def solution(mesh):
    in_specs = (
        P("ij", ("cd", "ab")),
        P(("ab", "cd"), None, None),
        P(("ab", "cd")),
        P(("ab", "cd")),
        P(("ab", "cd")),
    )
    out_specs = P("ij", "ab", "cd", None)
    return jax.shard_map(
        per_device, mesh=mesh, in_specs=in_specs, out_specs=out_specs, check_vma=False
    )
```

profile of v0, /device:TPU:0, one launch (start us, length us, event | category | flops | bytes accessed | tf_op | source)
XLA Modules:
  0.0 149.9 jit_solution(6584111835509438171)
XLA Ops:
  6.5 0.0 all-gather.2.cloned.1.call-start
  6.5 1.8 %copy.17 = f32[256,256]{0,1:T(8,128)} copy(f32[256,256]{1,0:T(8,128)} %param.5) | data formatting | bytes 524288 | tf_op args[0]
  8.3 0.0 all-gather.2.cloned.1.call-update
  8.3 0.0 reduce-scatter.2.cloned.1.call-start
  9.1 0.7 compare_select_fusion
  9.7 0.7 compare_and_fusion
  10.4 28.0 %all-gather.2.cloned.1.call-done = f32[256,1024]{0,1:T(8,128)} async-done(((f32[256,256]{0,1:T(8,128)}), f32[256,1024]{0,1:T(8,128)}) %all-gather.2.cloned.1.call-update) | async-done | bytes 1048592 | tf_op jit(solution)/shard_map/all_gather | solution.py:39
  38.4 1.6 %copy.18 = f32[256,4,256]{2,0,1:T(8,128)S(1)} copy(f32[256,4,256]{0,2,1:T(8,128)} %bitcast.34) | data formatting | bytes 2097152 | tf_op jit(solution)/shard_map/reshape | solution.py:40
  40.0 2.8 %gather_fusion = f32[16,256,256]{2,1,0:T(8,128)} fusion(f32[256,4,256]{2,0,1:T(8,128)S(1)} %copy.18, s32[1024]{0:T(1024)S(1)} %pad_clamp_fusion), kind=kCustom, calls=%fused_computation | custom fusion | bytes 8388672 | tf_op jit(solution)/shard_map/jit(_take)/gather | solution.py:41
  42.8 0.0 copy-start.1
  42.8 12.3 %fusion = f32[16,256,256]{1,2,0:T(8,128)S(1)} fusion(f32[16,256,256]{2,1,0:T(8,128)} %param.6, f32[16,256,256]{2,1,0:T(8,128)} %gather_fusion, pred[16]{0:T(512)(128)(4,1)S(1)} %compare_and_fusion), kind=kOutput, calls=%fused_computation.1 | convolution fusion | flops 3222274048 | bytes 12582928 | tf_op jit(solution)/shard_map/okf,kef->oke/dot_general | solution.py:19
  55.1 0.0 copy-done.1
  55.1 3.9 %fusion.7 = f32[16,256,4,16]{1,2,3,0:T(4,128)S(1)} fusion(f32[256,16,16,16]{0,3,2,1:T(8,128)S(1)} %bitcast.32, s32[16]{0:T(128)S(1)} %copy-done.1, pred[16]{0:T(512)(128)(4,1)S(1)} %iota_compare_fusion.1), kind=kOutput, calls=%fused_computation.8 | convolution fusion | flops 50331776 | bytes 5242960 | tf_op jit(solution)/shard_map/rk,okab->aorb/dot_general | solution.py:22
  58.9 1.2 copy.20
  60.1 0.0 reduce-scatter.2.cloned.1.call-update
  60.1 27.4 %reduce-scatter.2.cloned.1.call-done = f32[4,256,64]{1,2,0:T(8,128)} async-done(((f32[16,256,64]{1,2,0:T(8,128)}), f32[4,256,64]{1,2,0:T(8,128)}) %reduce-scatter.2.cloned.1.call-update) | async-done | bytes 262160 | tf_op jit(solution)/shard_map/reduce_scatter | solution.py:43
  87.6 1.0 reshape.39
  88.6 5.9 %copy.21 = f32[4,256,4,4,4]{4,0,1,3,2:T(4,128)} copy(f32[4,256,4,4,4]{1,4,3,2,0:T(4,128)S(1)} %reshape.39) | data formatting | bytes 524288 | tf_op jit(solution)/shard_map/reshape | solution.py:45
  94.5 11.3 %all_to_all.8 = f32[16,1,4096]{2,1,0:T(1,128)S(1)} reshape(f32[4,4,256,4,4]{4,3,2,1,0:T(4,128)} %bitcast.30) | data formatting | bytes 524288 | tf_op jit(solution)/shard_map/all_to_all | solution.py:47
  105.8 14.4 %all_to_all.10 = f32[16,1,4096]{2,1,0:T(1,128)S(1)} all-to-all(f32[16,1,4096]{2,1,0:T(1,128)S(1)} %all_to_all.8), channel_id=1, replica_groups=mesh['ab'=4,'cd'=4,'ij'=2] {'ab','cd'}, dimensions={0} | all-to-all | bytes 524288 | tf_op jit(solution)/shard_map/all_to_all | solution.py:47
  120.2 0.6 reduce
  120.8 12.9 %reshape.40 = f32[4,4,256,4,4]{4,3,2,1,0:T(4,128)} reshape(f32[16,4096]{1,0:T(8,128)S(1)} %reduce) | data formatting | bytes 524288 | tf_op jit(solution)/shard_map/reshape | solution.py:54
  133.7 0.0 copy-start
  133.7 6.9 %copy.23 = f32[256,4,4,4,4]{0,4,3,2,1:T(4,128)S(1)} copy(f32[256,4,4,4,4]{1,4,0,3,2:T(4,128)} %bitcast.31) | data formatting | bytes 524288 | tf_op jit(solution)/shard_map/transpose | solution.py:55
  140.6 0.1 reshape.41
  140.7 0.1 collective-permute-start
  140.8 1.5 %collective-permute-done = f32[256,4,64]{0,2,1:T(8,128)S(1)} collective-permute-done((f32[256,4,64]{0,2,1:T(8,128)S(1)}, f32[256,4,64]{0,2,1:T(8,128)S(1)}, u32[]{:S(2)}, u32[]{:S(2)}) %collective-permute-start) | collective-permute-done | bytes 262176 | tf_op jit(solution)/shard_map/ppermute | solution.py:15
  142.3 0.0 copy-done
  142.3 0.7 fusion.10
  (2 shorter events, 0.0 us)
Async XLA Ops:
  6.5 31.9 %all-gather.2.cloned.1.call-start = ((), (), s32[]{:S(2)}) async-start(), calls=%async_computation.2 | async-start | bytes 1310720 | tf_op jit(solution)/shard_map/all_gather | solution.py:39
  8.3 79.2 %reduce-scatter.2.cloned.1.call-start = ((), (), s32[]{:S(2)}) async-start(), calls=%async_computation.3 | async-start | bytes 1310720 | tf_op jit(solution)/shard_map/reduce_scatter | solution.py:43
  42.8 12.3 %copy-start.1 = (s32[16]{0:T(128)S(1)}, s32[16]{0:T(128)}, u32[]{:S(2)}) copy-start(s32[16]{0:T(128)} %param.7) | copy-start | bytes 196
  133.7 8.6 %copy-start = (f32[4,256,64]{1,2,0:T(8,128)S(1)}, f32[4,256,64]{1,2,0:T(8,128)}, u32[]{:S(2)}) copy-start(f32[4,256,64]{1,2,0:T(8,128)} %reduce-scatter.2.cloned.1.call-done) | copy-start | bytes 786436
  140.7 1.6 %collective-permute-start = (f32[256,4,64]{0,2,1:T(8,128)S(1)}, f32[256,4,64]{0,2,1:T(8,128)S(1)}, u32[]{:S(2)}, u32[]{:S(2)}) collective-permute-start(f32[256,4,64]{0,2,1:T(8,128)S(1)} %reshape.41), channel_id=1, source_target_pairs={{0,1},{1,0},{2,3},{3,2},{4,5},{5,4},{6,7},{7,6},{8,9},{9,8},{10,11... | collective-permute-start | bytes 786440 | tf_op jit(solution)/shard_map/ppermute | solution.py:15
Sparse Core Ops, SparseCore 0:
  9.2 29.2 all-gather.1
  60.2 27.2 reduce-scatter.1
where the time goes:
time: 150 us
  waiting for transfers between devices  57 us (38%)
  local copies, waits for them, and re-layouts  45.3 us (30%)
  matrix products  16.2 us (11%)
  blocking collectives  14.4 us (10%)
  between operations  14.1 us (9%)
  other arithmetic  2.69 us (2%)
    all_gather x1, waiting for transfers between devices, per_device(): gathered = lax.all_gather(amplitudes, 'ab', axis=1, tiled=True)  28 us
    reduce_scatter x1, waiting for transfers between devices, per_device(): lax.psum_scatter(partial_value, 'cd', scatter_dimension=0, tiled=True)  27.4 us
    all_to_all x1, blocking collectives, per_device(): lax.all_to_all(outgoing.reshape(blocks * cd_size, occ_dev * group_size *...  14.4 us
    reshape x1, local copies, waits for them, and re-layouts, per_device(): arrived = arrived.reshape(blocks, cd_size, occ_dev, group_size, group_size)  12.9 us
    dot_general x1, matrix products, place_rows(): jnp.einsum('okf,kef->oke', chosen, tile_rows, precision=lax.Precision.HIG...  12.3 us
    all_to_all x1, local copies, waits for them, and re-layouts, per_device(): lax.all_to_all(outgoing.reshape(blocks * cd_size, occ_dev * group_size *...  11.3 us
    reshape x2, local copies, waits for them, and re-layouts, per_device(): outgoing = summed.reshape(group_size, occ_dev, blocks, cd_size, group_size)  6.91 us
    transpose x1, local copies, waits for them, and re-layouts, per_device(): jnp.transpose(arrived, (2, 4, 0, 1, 3))  6.88 us
  transfers between devices with their start and end apart: 3, of which 3 were waited for; matrix products, arithmetic and copies ran while one was open for 1% of the time, Pallas kernels for 0%

commit v1 on v0

--- a/solution.py
+++ b/solution.py
@@ -3,6 +3,18 @@
 import jax.numpy as jnp
 from jax import lax
 from jax.sharding import PartitionSpec as P
+
+
+def cut_along(array, dim, devices):
+    shape = array.shape
+    tiles = array.reshape(*shape[:dim], devices, shape[dim] // devices, *shape[dim + 1 :])
+    return jnp.moveaxis(tiles, dim, 0)
+
+
+def in_order(pieces, dim):
+    shape = list(pieces.shape[1:])
+    shape[dim] *= pieces.shape[0]
+    return jnp.moveaxis(pieces, 0, dim).reshape(shape)
 
 
 def from_partner(block, axis, bit):
@@ -44,13 +56,15 @@
     direct = jnp.transpose(summed, (1, 0, 2))
     outgoing = summed.reshape(group_size, occ_dev, blocks, cd_size, group_size)
     outgoing = jnp.transpose(outgoing, (2, 3, 1, 0, 4))
-    arrived = lax.all_to_all(
-        outgoing.reshape(blocks * cd_size, occ_dev * group_size * group_size),
-        ("ab", "cd"),
-        split_axis=0,
-        concat_axis=0,
-        tiled=True,
-    )
+    x = outgoing.reshape(blocks * cd_size, occ_dev * group_size * group_size)
+    size, index = (lax.axis_size(("ab", "cd")), lax.axis_index(("ab", "cd")))
+    blocks_2 = cut_along(x, 0, size)
+    finished = [blocks_2[index]]
+    for turn in range(1, size):
+        sent = blocks_2[index ^ turn]
+        finished.append(lax.ppermute(sent, ("ab", "cd"), [(i, i ^ turn) for i in range(size)]))
+    blocks_2 = jnp.stack(finished)[index ^ jnp.arange(size)]
+    arrived = in_order(blocks_2, 0)
     arrived = arrived.reshape(blocks, cd_size, occ_dev, group_size, group_size)
     mirrored = jnp.transpose(arrived, (2, 4, 0, 1, 3)).reshape(
         occ_dev, group_size, blocks * block_size

time: 150 us -> 169 us (1.13)
  starting transfers between devices: 0.11 us -> 26.7 us
  blocking collectives: 14.4 us -> 0 us
  waiting for transfers between devices: 57 us -> 61.4 us
  local copies, waits for them, and re-layouts: 45.3 us -> 47.8 us
    ppermute x0 -> x15, starting transfers between devices: none -> 26.5 us  [per_device(): lax.ppermute(sent, ('ab', 'cd'), [(i, i ^ turn) for i in range(size)])]
    another operation x0 -> x3, local copies, waits for them, and re-layouts: none -> 25.6 us  [the longest x1 12.9 us: per_device(): arrived = arrived.reshape(blocks, cd_size, occ_dev, group_size, group_size)]
    all_to_all x1 -> x0, blocking collectives: 14.4 us -> none  [per_device(): lax.all_to_all(outgoing.reshape(blocks * cd_size, occ_dev * group_size *...]
    reshape x1 -> x0, local copies, waits for them, and re-layouts: 12.9 us -> none  [per_device(): arrived = arrived.reshape(blocks, cd_size, occ_dev, group_size, group_size)]
    all_to_all x1 -> x0, local copies, waits for them, and re-layouts: 11.3 us -> none  [per_device(): lax.all_to_all(outgoing.reshape(blocks * cd_size, occ_dev * group_size *...]
    ppermute x0 -> x15, waiting for transfers between devices: none -> 4.43 us  [per_device(): lax.ppermute(sent, ('ab', 'cd'), [(i, i ^ turn) for i in range(size)])]
  transfers between devices with their start and end apart: 3 -> 18, of which waited for: 3 -> 5; matrix products, arithmetic and copies ran while one was open for 1% -> 1% of each run, Pallas kernels for 0% -> 0%
where the time goes in v1:
time: 169 us; the launch traced here: 168 us
  waiting for transfers between devices  61.4 us (36%)
  local copies, waits for them, and re-layouts  47.8 us (28%)
  starting transfers between devices  26.7 us (16%)
  matrix products  16.1 us (10%)
  between operations  14.3 us (8%)
  other arithmetic  2.09 us (1%)
    all_gather x1, waiting for transfers between devices, per_device(): gathered = lax.all_gather(amplitudes, 'ab', axis=1, tiled=True)  28 us
    reduce_scatter x1, waiting for transfers between devices, per_device(): lax.psum_scatter(partial_value, 'cd', scatter_dimension=0, tiled=True)  27.4 us
    ppermute x15, starting transfers between devices, per_device(): lax.ppermute(sent, ('ab', 'cd'), [(i, i ^ turn) for i in range(size)])  26.5 us
    another operation x1, local copies, waits for them, and re-layouts, per_device(): arrived = arrived.reshape(blocks, cd_size, occ_dev, group_size, group_size)  12.9 us
    another operation x1, local copies, waits for them, and re-layouts, cut_along(): array.reshape(*shape[:dim], devices, shape[dim] // devices, *shape[dim +...  12.3 us
    dot_general x1, matrix products, place_rows(): jnp.einsum('okf,kef->oke', chosen, tile_rows, precision=lax.Precision.HIG...  12.3 us
    reshape x2, local copies, waits for them, and re-layouts, per_device(): outgoing = summed.reshape(group_size, occ_dev, blocks, cd_size, group_size)  6.95 us
    transpose x1, local copies, waits for them, and re-layouts, per_device(): jnp.transpose(arrived, (2, 4, 0, 1, 3))  6.88 us
  transfers between devices with their start and end apart: 18, of which 5 were waited for; matrix products, arithmetic and copies ran while one was open for 1% of the time, Pallas kernels for 0%

profile of v1, /device:TPU:0, one launch (start us, length us, event | category | flops | bytes accessed | tf_op | source)
XLA Modules:
  0.0 168.3 jit_solution(14620065206130452820)
XLA Ops:
  6.5 1.8 %copy.13 = f32[256,256]{0,1:T(8,128)} copy(f32[256,256]{1,0:T(8,128)} %param.5) | data formatting | bytes 524288 | tf_op args[0]
  8.3 0.0 all-gather.2.cloned.1.call-update
  8.3 0.0 reduce-scatter.2.cloned.1.call-start
  9.1 0.7 compare_select_fusion.1
  9.7 0.7 compare_and_fusion
  10.4 28.0 %all-gather.2.cloned.1.call-done = f32[256,1024]{0,1:T(8,128)} async-done(((f32[256,256]{0,1:T(8,128)}), f32[256,1024]{0,1:T(8,128)}) %all-gather.2.cloned.1.call-update) | async-done | bytes 1048592 | tf_op jit(solution)/shard_map/all_gather | solution.py:51
  38.4 1.6 copy.14
  40.0 2.8 %gather_fusion = f32[16,256,256]{2,1,0:T(8,128)} fusion(f32[256,4,256]{2,0,1:T(8,128)S(1)} %copy.14, s32[1024]{0:T(1024)S(1)} %pad_clamp_fusion.1), kind=kCustom, calls=%fused_computation | custom fusion | bytes 8388672 | tf_op jit(solution)/shard_map/jit(_take)/gather | solution.py:53
  42.7 12.3 %fusion = f32[16,256,256]{1,2,0:T(8,128)S(1)} fusion(f32[16,256,256]{2,1,0:T(8,128)} %param.6, f32[16,256,256]{2,1,0:T(8,128)} %gather_fusion, pred[16]{0:T(512)(128)(4,1)S(1)} %compare_and_fusion), kind=kOutput, calls=%fused_computation.2 | convolution fusion | flops 3222274048 | bytes 12582928 | tf_op jit(solution)/shard_map/okf,kef->oke/dot_general | solution.py:31
  55.0 3.9 %fusion.7 = f32[16,256,4,16]{1,2,3,0:T(4,128)S(1)} fusion(f32[256,16,16,16]{0,3,2,1:T(8,128)S(1)} %bitcast.81, s32[16]{0:T(128)S(1)} %copy-done.1, pred[16]{0:T(512)(128)(4,1)S(1)} %iota_compare_fusion.1), kind=kOutput, calls=%fused_computation.9 | convolution fusion | flops 50331776 | bytes 5242960 | tf_op jit(solution)/shard_map/rk,okab->aorb/dot_general | solution.py:34
  58.9 1.2 copy.16
  60.1 0.0 reduce-scatter.2.cloned.1.call-update
  60.2 27.4 %reduce-scatter.2.cloned.1.call-done = f32[4,256,64]{1,2,0:T(8,128)} async-done(((f32[16,256,64]{1,2,0:T(8,128)}), f32[4,256,64]{1,2,0:T(8,128)}) %reduce-scatter.2.cloned.1.call-update) | async-done | bytes 262160 | tf_op jit(solution)/shard_map/reduce_scatter | solution.py:55
  87.6 1.0 reshape.47
  88.6 5.9 %copy.17 = f32[4,256,4,4,4]{4,0,1,3,2:T(4,128)} copy(f32[4,256,4,4,4]{1,4,3,2,0:T(4,128)S(1)} %reshape.47) | data formatting | bytes 524288 | tf_op jit(solution)/shard_map/reshape | solution.py:57
  94.5 12.3 %reshape_reshape.6 = f32[16,1,4096]{2,0,1:T(8,128)S(1)} reshape(f32[4,4,256,4,4]{4,3,2,1,0:T(4,128)} %bitcast.78) | data formatting | bytes 524288 | tf_op jit(solution)/shard_map/reshape;reshape | solution.py:10
  106.9 0.3 dynamic-slice_bitcast_fusion
  107.2 0.1 collective-permute-start
  107.3 1.4 collective-permute-start.1
  108.7 2.9 %collective-permute-start.2 = (f32[1,4096]{1,0:T(1,128)S(1)}, f32[1,4096]{1,0:T(1,128)S(1)}, u32[]{:S(2)}, u32[]{:S(2)}) collective-permute-start(f32[1,4096]{1,0:T(1,128)S(1)} %get-tuple-element.17), channel_id=1, source_target_pairs={{0,6},{2,4},{4,2},{6,0},{8,14},{10,12},{12,10},{14,8},{16,22},{18,... | collective-permute-start | bytes 49160 | tf_op jit(solution)/shard_map/ppermute | solution.py:65
  111.6 1.5 collective-permute-start.3
  113.1 0.0 collective-permute-start.4
  113.1 2.4 %collective-permute-start.5 = (f32[1,4096]{1,0:T(1,128)S(1)}, f32[1,4096]{1,0:T(1,128)S(1)}, u32[]{:S(2)}, u32[]{:S(2)}) collective-permute-start(f32[1,4096]{1,0:T(1,128)S(1)} %get-tuple-element.14), channel_id=1, source_target_pairs={{0,12},{2,14},{4,8},{6,10},{8,4},{10,6},{12,0},{14,2},{16,28},{18,... | collective-permute-start | bytes 49160 | tf_op jit(solution)/shard_map/ppermute | solution.py:65
  115.5 0.0 collective-permute-done.1
  115.5 2.9 %collective-permute-start.6 = (f32[1,4096]{1,0:T(1,128)S(1)}, f32[1,4096]{1,0:T(1,128)S(1)}, u32[]{:S(2)}, u32[]{:S(2)}) collective-permute-start(f32[1,4096]{1,0:T(1,128)S(1)} %get-tuple-element.13), channel_id=1, source_target_pairs={{0,14},{2,12},{4,10},{6,8},{8,6},{10,4},{12,2},{14,0},{16,30},{18,... | collective-permute-start | bytes 49160 | tf_op jit(solution)/shard_map/ppermute | solution.py:65
  118.4 0.0 collective-permute-done.2
  118.4 1.5 collective-permute-start.7
  119.9 0.0 collective-permute-done.3
  119.9 0.0 collective-permute-start.8
  119.9 2.4 %collective-permute-start.9 = (f32[1,4096]{1,0:T(1,128)S(1)}, f32[1,4096]{1,0:T(1,128)S(1)}, u32[]{:S(2)}, u32[]{:S(2)}) collective-permute-start(f32[1,4096]{1,0:T(1,128)S(1)} %get-tuple-element.10), channel_id=1, source_target_pairs={{0,20},{2,22},{4,16},{6,18},{8,28},{10,30},{12,24},{14,26},{16,4},... | collective-permute-start | bytes 49160 | tf_op jit(solution)/shard_map/ppermute | solution.py:65
  122.3 0.0 collective-permute-done.5
  122.3 3.0 %collective-permute-start.10 = (f32[1,4096]{1,0:T(1,128)S(1)}, f32[1,4096]{1,0:T(1,128)S(1)}, u32[]{:S(2)}, u32[]{:S(2)}) collective-permute-start(f32[1,4096]{1,0:T(1,128)S(1)} %get-tuple-element.9), channel_id=1, source_target_pairs={{0,22},{2,20},{4,18},{6,16},{8,30},{10,28},{12,26},{14,24},{16,6},... | collective-permute-start | bytes 49160 | tf_op jit(solution)/shard_map/ppermute | solution.py:65
  125.2 0.0 collective-permute-done.6
  125.2 2.4 %collective-permute-start.11 = (f32[1,4096]{1,0:T(1,128)S(1)}, f32[1,4096]{1,0:T(1,128)S(1)}, u32[]{:S(2)}, u32[]{:S(2)}) collective-permute-start(f32[1,4096]{1,0:T(1,128)S(1)} %get-tuple-element.8), channel_id=1, source_target_pairs={{0,24},{2,26},{4,28},{6,30},{8,16},{10,18},{12,20},{14,22},{16,8},... | collective-permute-start | bytes 49160 | tf_op jit(solution)/shard_map/ppermute | solution.py:65
  127.6 3.2 %collective-permute-start.13 = (f32[1,4096]{1,0:T(1,128)S(1)}, f32[1,4096]{1,0:T(1,128)S(1)}, u32[]{:S(2)}, u32[]{:S(2)}) collective-permute-start(f32[1,4096]{1,0:T(1,128)S(1)} %get-tuple-element.6), channel_id=1, source_target_pairs={{0,28},{2,30},{4,24},{6,26},{8,20},{10,22},{12,16},{14,18},{16,12}... | collective-permute-start | bytes 49160 | tf_op jit(solution)/shard_map/ppermute | solution.py:65
  130.9 0.0 collective-permute-done.9
  130.9 2.9 %collective-permute-start.14 = (f32[1,4096]{1,0:T(1,128)S(1)}, f32[1,4096]{1,0:T(1,128)S(1)}, u32[]{:S(2)}, u32[]{:S(2)}) collective-permute-start(f32[1,4096]{1,0:T(1,128)S(1)} %get-tuple-element.5), channel_id=1, source_target_pairs={{0,30},{2,28},{4,26},{6,24},{8,22},{10,20},{12,18},{14,16},{16,14}... | collective-permute-start | bytes 49160 | tf_op jit(solution)/shard_map/ppermute | solution.py:65
  133.8 0.0 collective-permute-done.11
  133.8 0.3 collective-permute-done.13
  134.1 4.1 %collective-permute-done.14 = f32[1,4096]{1,0:T(1,128)S(1)} collective-permute-done((f32[1,4096]{1,0:T(1,128)S(1)}, f32[1,4096]{1,0:T(1,128)S(1)}, u32[]{:S(2)}, u32[]{:S(2)}) %collective-permute-start.14) | collective-permute-done | bytes 16416 | tf_op jit(solution)/shard_map/ppermute | solution.py:65
  138.2 0.4 stack.63
  138.6 0.6 gather_fusion.1
  139.2 12.9 %reshape_reshape.7 = f32[4,4,256,4,4]{4,3,2,1,0:T(4,128)} reshape(f32[16,4096]{1,0:T(8,128)S(1)} %gather_fusion.1) | data formatting | bytes 524288 | tf_op jit(solution)/shard_map/reshape;reshape | solution.py:68
  152.1 6.9 %copy.18 = f32[256,4,4,4,4]{0,4,3,2,1:T(4,128)S(1)} copy(f32[256,4,4,4,4]{1,4,0,3,2:T(4,128)} %bitcast.79) | data formatting | bytes 524288 | tf_op jit(solution)/shard_map/transpose | solution.py:69
  159.0 0.1 reshape.48
  159.1 0.1 collective-permute-start.15
  159.2 1.5 collective-permute-done.15
  160.7 0.7 fusion.10
  (16 shorter events, 0.1 us)
Async XLA Ops:
  6.5 31.9 %all-gather.2.cloned.1.call-start = ((), (), s32[]{:S(2)}) async-start(), calls=%async_computation.1 | async-start | bytes 1310720 | tf_op jit(solution)/shard_map/all_gather | solution.py:51
  8.3 79.2 %reduce-scatter.2.cloned.1.call-start = ((), (), s32[]{:S(2)}) async-start(), calls=%async_computation.2 | async-start | bytes 1310720 | tf_op jit(solution)/shard_map/reduce_scatter | solution.py:55
  42.7 12.3 %copy-start.1 = (s32[16]{0:T(128)S(1)}, s32[16]{0:T(128)}, u32[]{:S(2)}) copy-start(s32[16]{0:T(128)} %param.7) | copy-start | bytes 196
  107.2 5.9 %collective-permute-start = (f32[1,4096]{1,0:T(1,128)S(1)}, f32[1,4096]{1,0:T(1,128)S(1)}, u32[]{:S(2)}, u32[]{:S(2)}) collective-permute-start(f32[1,4096]{1,0:T(1,128)S(1)} %get-tuple-element.19), channel_id=1, source_target_pairs={{0,2},{2,0},{4,6},{6,4},{8,10},{10,8},{12,14},{14,12},{16,18},{18,... | collective-permute-start | bytes 49160 | tf_op jit(solution)/shard_map/ppermute | solution.py:65
  107.3 8.2 %collective-permute-start.1 = (f32[1,4096]{1,0:T(1,128)S(1)}, f32[1,4096]{1,0:T(1,128)S(1)}, u32[]{:S(2)}, u32[]{:S(2)}) collective-permute-start(f32[1,4096]{1,0:T(1,128)S(1)} %get-tuple-element.18), channel_id=1, source_target_pairs={{0,4},{2,6},{4,0},{6,2},{8,12},{10,14},{12,8},{14,10},{16,20},{18,... | collective-permute-start | bytes 49160 | tf_op jit(solution)/shard_map/ppermute | solution.py:65
  108.7 9.7 %collective-permute-start.2 = (f32[1,4096]{1,0:T(1,128)S(1)}, f32[1,4096]{1,0:T(1,128)S(1)}, u32[]{:S(2)}, u32[]{:S(2)}) collective-permute-start(f32[1,4096]{1,0:T(1,128)S(1)} %get-tuple-element.17), channel_id=1, source_target_pairs={{0,6},{2,4},{4,2},{6,0},{8,14},{10,12},{12,10},{14,8},{16,22},{18,... | collective-permute-start | bytes 49160 | tf_op jit(solution)/shard_map/ppermute | solution.py:65
  111.6 8.2 %collective-permute-start.3 = (f32[1,4096]{1,0:T(1,128)S(1)}, f32[1,4096]{1,0:T(1,128)S(1)}, u32[]{:S(2)}, u32[]{:S(2)}) collective-permute-start(f32[1,4096]{1,0:T(1,128)S(1)} %get-tuple-element.16), channel_id=1, source_target_pairs={{0,8},{2,10},{4,12},{6,14},{8,0},{10,2},{12,4},{14,6},{16,24},{18,... | collective-permute-start | bytes 49160 | tf_op jit(solution)/shard_map/ppermute | solution.py:65
  113.1 6.8 %collective-permute-start.4 = (f32[1,4096]{1,0:T(1,128)S(1)}, f32[1,4096]{1,0:T(1,128)S(1)}, u32[]{:S(2)}, u32[]{:S(2)}) collective-permute-start(f32[1,4096]{1,0:T(1,128)S(1)} %get-tuple-element.15), channel_id=1, source_target_pairs={{0,10},{2,8},{4,14},{6,12},{8,2},{10,0},{12,6},{14,4},{16,26},{18,... | collective-permute-start | bytes 49160 | tf_op jit(solution)/shard_map/ppermute | solution.py:65
  113.1 9.2 %collective-permute-start.5 = (f32[1,4096]{1,0:T(1,128)S(1)}, f32[1,4096]{1,0:T(1,128)S(1)}, u32[]{:S(2)}, u32[]{:S(2)}) collective-permute-start(f32[1,4096]{1,0:T(1,128)S(1)} %get-tuple-element.14), channel_id=1, source_target_pairs={{0,12},{2,14},{4,8},{6,10},{8,4},{10,6},{12,0},{14,2},{16,28},{18,... | collective-permute-start | bytes 49160 | tf_op jit(solution)/shard_map/ppermute | solution.py:65
  115.5 9.8 %collective-permute-start.6 = (f32[1,4096]{1,0:T(1,128)S(1)}, f32[1,4096]{1,0:T(1,128)S(1)}, u32[]{:S(2)}, u32[]{:S(2)}) collective-permute-start(f32[1,4096]{1,0:T(1,128)S(1)} %get-tuple-element.13), channel_id=1, source_target_pairs={{0,14},{2,12},{4,10},{6,8},{8,6},{10,4},{12,2},{14,0},{16,30},{18,... | collective-permute-start | bytes 49160 | tf_op jit(solution)/shard_map/ppermute | solution.py:65
  118.4 9.2 %collective-permute-start.7 = (f32[1,4096]{1,0:T(1,128)S(1)}, f32[1,4096]{1,0:T(1,128)S(1)}, u32[]{:S(2)}, u32[]{:S(2)}) collective-permute-start(f32[1,4096]{1,0:T(1,128)S(1)} %get-tuple-element.12), channel_id=1, source_target_pairs={{0,16},{2,18},{4,20},{6,22},{8,24},{10,26},{12,28},{14,30},{16,0},... | collective-permute-start | bytes 49160 | tf_op jit(solution)/shard_map/ppermute | solution.py:65
  119.9 7.8 %collective-permute-start.8 = (f32[1,4096]{1,0:T(1,128)S(1)}, f32[1,4096]{1,0:T(1,128)S(1)}, u32[]{:S(2)}, u32[]{:S(2)}) collective-permute-start(f32[1,4096]{1,0:T(1,128)S(1)} %get-tuple-element.11), channel_id=1, source_target_pairs={{0,18},{2,16},{4,22},{6,20},{8,26},{10,24},{12,30},{14,28},{16,2},... | collective-permute-start | bytes 49160 | tf_op jit(solution)/shard_map/ppermute | solution.py:65
  119.9 11.0 %collective-permute-start.9 = (f32[1,4096]{1,0:T(1,128)S(1)}, f32[1,4096]{1,0:T(1,128)S(1)}, u32[]{:S(2)}, u32[]{:S(2)}) collective-permute-start(f32[1,4096]{1,0:T(1,128)S(1)} %get-tuple-element.10), channel_id=1, source_target_pairs={{0,20},{2,22},{4,16},{6,18},{8,28},{10,30},{12,24},{14,26},{16,4},... | collective-permute-start | bytes 49160 | tf_op jit(solution)/shard_map/ppermute | solution.py:65
  122.3 11.5 %collective-permute-start.10 = (f32[1,4096]{1,0:T(1,128)S(1)}, f32[1,4096]{1,0:T(1,128)S(1)}, u32[]{:S(2)}, u32[]{:S(2)}) collective-permute-start(f32[1,4096]{1,0:T(1,128)S(1)} %get-tuple-element.9), channel_id=1, source_target_pairs={{0,22},{2,20},{4,18},{6,16},{8,30},{10,28},{12,26},{14,24},{16,6},... | collective-permute-start | bytes 49160 | tf_op jit(solution)/shard_map/ppermute | solution.py:65
  125.2 8.6 %collective-permute-start.11 = (f32[1,4096]{1,0:T(1,128)S(1)}, f32[1,4096]{1,0:T(1,128)S(1)}, u32[]{:S(2)}, u32[]{:S(2)}) collective-permute-start(f32[1,4096]{1,0:T(1,128)S(1)} %get-tuple-element.8), channel_id=1, source_target_pairs={{0,24},{2,26},{4,28},{6,30},{8,16},{10,18},{12,20},{14,22},{16,8},... | collective-permute-start | bytes 49160 | tf_op jit(solution)/shard_map/ppermute | solution.py:65
  127.6 6.2 %collective-permute-start.12 = (f32[1,4096]{1,0:T(1,128)S(1)}, f32[1,4096]{1,0:T(1,128)S(1)}, u32[]{:S(2)}, u32[]{:S(2)}) collective-permute-start(f32[1,4096]{1,0:T(1,128)S(1)} %get-tuple-element.7), channel_id=1, source_target_pairs={{0,26},{2,24},{4,30},{6,28},{8,18},{10,16},{12,22},{14,20},{16,10}... | collective-permute-start | bytes 49160 | tf_op jit(solution)/shard_map/ppermute | solution.py:65
  127.6 6.5 %collective-permute-start.13 = (f32[1,4096]{1,0:T(1,128)S(1)}, f32[1,4096]{1,0:T(1,128)S(1)}, u32[]{:S(2)}, u32[]{:S(2)}) collective-permute-start(f32[1,4096]{1,0:T(1,128)S(1)} %get-tuple-element.6), channel_id=1, source_target_pairs={{0,28},{2,30},{4,24},{6,26},{8,20},{10,22},{12,16},{14,18},{16,12}... | collective-permute-start | bytes 49160 | tf_op jit(solution)/shard_map/ppermute | solution.py:65
  130.9 7.3 %collective-permute-start.14 = (f32[1,4096]{1,0:T(1,128)S(1)}, f32[1,4096]{1,0:T(1,128)S(1)}, u32[]{:S(2)}, u32[]{:S(2)}) collective-permute-start(f32[1,4096]{1,0:T(1,128)S(1)} %get-tuple-element.5), channel_id=1, source_target_pairs={{0,30},{2,28},{4,26},{6,24},{8,22},{10,20},{12,18},{14,16},{16,14}... | collective-permute-start | bytes 49160 | tf_op jit(solution)/shard_map/ppermute | solution.py:65
  152.1 8.6 %copy-start = (f32[4,256,64]{1,2,0:T(8,128)S(1)}, f32[4,256,64]{1,2,0:T(8,128)}, u32[]{:S(2)}) copy-start(f32[4,256,64]{1,2,0:T(8,128)} %reduce-scatter.2.cloned.1.call-done) | copy-start | bytes 786436
  159.1 1.6 collective-permute-start.15
Sparse Core Ops, SparseCore 0:
  9.2 29.2 all-gather.1
  60.2 27.3 reduce-scatter.1
